TPU v7x, 256 devices: a whole 4x4x8 slice. The times are simulated.
256 devices in a mesh: rows: 8 (over x, core), pts: 32 (over y, z).
Axes of the slice: x: 4, y: 4, z: 8, core: 2. Of those that a mesh axis runs over, the one named last changes fastest.
Arguments:
- features: bfloat16 [32768, 128], P('pts'), may hold values from -6 to 6
- targets: bfloat16 [32768, 256], P('pts'), may hold values from -6 to 6
- coefficients: float32 [32768, 256], P('pts'), may hold values from -6 to 6
- momentum: float32 [32768, 256], P('pts'), may hold values from -6 to 6
- block_index: int32 [2, 2048], replicated, may hold values from 0 to 32767, as said below
- pivot_index: int32 [2, 512], replicated, may hold values from 0 to 2047, as said below
- nystrom_core: bfloat16 [2, 512, 512], replicated, may hold values from -0.5 to 3
Outputs:
- new_coefficients: float32 [32768, 256], P('pts')
- new_momentum: float32 [32768, 256], P('pts')
Inputs may be any that keep to these rules, and one draw needn't show every extreme that they name: `block_index`: each row lists 2048 distinct points; a point p belongs to index p // 1024 of pts; in each row one index of pts, drawn from the seed, owns exactly 24 of the points in every aligned group of 256 positions, and no index owns more than 24 points of any such group. `pivot_index`: each row lists 512 distinct positions.
All inputs are finite; a program needn't handle non-finite values.
Results may differ from a plain program's by a relative error of at most 0.0041.
The roundings to bfloat16 on the way count: a program that leaves them out, or rounds other values in their place, can miss the bound.
Values may be sent and summed in bfloat16 or wider, within the bound.
A program may use at most 64 MiB of HBM per device.

v0:
```python
import jax
import jax.numpy as jnp
from jax import lax
from jax.sharding import PartitionSpec as P

UPDATES = 2
alpha_mix = 0.6
beta_keep = 0.9
step_size = 0.2
momentum_gain = 1.5
ridge_term = 1.0


def kernel_tile(left_rows, right_rows):
    inner_prod = lax.dot_general(
        left_rows, right_rows, (((1,), (1,)), ((), ())), preferred_element_type=jnp.float32
    )
    left_sq = jnp.sum(jnp.square(left_rows.astype(jnp.float32)), axis=1)
    right_sq = jnp.sum(jnp.square(right_rows.astype(jnp.float32)), axis=1)
    squared = left_sq[:, None] + right_sq[None, :] - 2.0 * inner_prod
    return jnp.exp(squared * (-3.5 / left_rows.shape[1])).astype(jnp.bfloat16)


def project_rows(factor, resid):
    return lax.dot_general(
        factor,
        resid.astype(jnp.bfloat16),
        (((0,), (0,)), ((), ())),
        preferred_element_type=jnp.float32,
    )


def finish_step(resid, factor, proj, core_now):
    lifted = jnp.dot(
        core_now, proj.astype(jnp.bfloat16), preferred_element_type=jnp.float32
    ).astype(jnp.bfloat16)
    return (resid - jnp.dot(factor, lifted, preferred_element_type=jnp.float32)).astype(
        jnp.bfloat16
    )


def owned_rows(local_feats, wanted, first_point):
    local_pos = wanted - first_point
    holder = (local_pos >= 0) & (local_pos < local_feats.shape[0])
    safe_pos = jnp.clip(local_pos, 0, local_feats.shape[0] - 1)
    return (holder, safe_pos)


def shards(features, targets, coefficients, momentum, block_index, pivot_index, nystrom_core):
    row_count = lax.axis_size("rows")
    pts_count = lax.axis_size("pts")
    row_id = lax.axis_index("rows")
    pts_id = lax.axis_index("pts")
    local_points = features.shape[0]
    per_row = block_index.shape[1] // row_count
    per_device = per_row // pts_count
    first_point = pts_id * local_points
    current = coefficients
    momentum_now = momentum
    for update in range(UPDATES):
        mixed = alpha_mix * momentum_now + (1.0 - alpha_mix) * current
        mixed_bf = mixed.astype(jnp.bfloat16)
        whole_index = block_index[update]
        row_points = lax.dynamic_slice_in_dim(whole_index, row_id * per_row, per_row)
        holder, safe_pos = owned_rows(features, row_points, first_point)
        row_terms = jnp.where(holder[:, None], features[safe_pos], jnp.zeros((), jnp.bfloat16))
        offset = jnp.where(
            holder[:, None],
            ridge_term * mixed[safe_pos] - targets[safe_pos].astype(jnp.float32),
            0.0,
        )
        pivot_points = whole_index[pivot_index[update]]
        pivot_holder, pivot_pos = owned_rows(features, pivot_points, first_point)
        pivot_terms = jnp.where(
            pivot_holder[:, None], features[pivot_pos], jnp.zeros((), jnp.bfloat16)
        )
        got_rows, got_pivots = (
            lax.psum(row_terms, "pts").astype(jnp.float32),
            lax.psum(pivot_terms, "pts").astype(jnp.float32),
        )
        block_feats = got_rows.astype(jnp.bfloat16)
        pivot_feats = got_pivots.astype(jnp.bfloat16)
        partial_value = (
            jnp.dot(
                kernel_tile(block_feats, features), mixed_bf, preferred_element_type=jnp.float32
            )
            + offset
        )
        local_all = whole_index - first_point
        whole_slots = jnp.where(
            (local_all >= 0) & (local_all < local_points), local_all, local_points
        )
        resid = lax.psum_scatter(partial_value, "pts", scatter_dimension=0, tiled=True)
        share_feats = lax.dynamic_slice_in_dim(block_feats, pts_id * per_device, per_device)
        factor = kernel_tile(share_feats, pivot_feats)
        proj = lax.psum(project_rows(factor, resid), ("rows", "pts"))
        step_bf = finish_step(resid, factor, proj, nystrom_core[update])
        steps = lax.all_gather(step_bf, ("rows", "pts"), axis=0, tiled=True)
        change = steps.astype(jnp.float32)
        current = mixed.at[whole_slots].add(-step_size * change, mode="drop")
        momentum_now = (
            (beta_keep * momentum_now + (1.0 - beta_keep) * mixed)
            .at[whole_slots]
            .add(-step_size * momentum_gain * change, mode="drop")
        )
    return (current, momentum_now)


def solution(mesh):
    in_specs = (P("pts", None), P("pts", None), P("pts", None), P("pts", None), P(), P(), P())
    out_specs = (P("pts", None), P("pts", None))
    return jax.shard_map(shards, mesh=mesh, in_specs=in_specs, out_specs=out_specs, check_vma=False)
```

profile of v0, /device:TPU:1, one launch (start us, length us, event | category | flops | bytes accessed | tf_op | source)
XLA Modules:
  0.0 1027.0 jit_solution(4563416117021022142)
XLA Ops:
  7.2 0.8 fusion.70
  8.9 3.1 gather_fusion.8
  12.1 3.1 gather_fusion.3
  15.3 0.9 gather_fusion
  16.2 1.3 gather_fusion.4
  17.5 0.9 gather_fusion.5
  18.4 1.3 gather_fusion.9
  22.9 2.6 multiply_add_fusion.2
  25.4 1.0 gather_fusion.1
  26.4 1.2 gather_fusion.2
  27.8 140.3 %all-reduce.5.cloned.1.call-done = (bf16[256,128]{1,0:T(8,128)(2,1)}, bf16[512,128]{1,0:T(8,128)(2,1)}, bf16[256,128]{1,0:T(8,128)(2,1)}, bf16[512,128]{1,0:T(8,128)(2,1)}) async-done(((bf16[256,128]{1,0:T(8,128)(2,1)}, bf16[512,128]{1,0:T(8,128)(2,1)}, bf16[256,128]{1,0:T(8,128)(2,1)}, bf16[512,128]{1,0:T(8,128)(2,1)}), (bf16[256,128]{1,0:T(8,128)(2,1)}, bf16[512,128]{1,0:T(8,128)(2,1)}, ...) | async-done | bytes 393232 | tf_op jit(solution)/shard_map/psum | solution.py:78
  168.1 0.9 multiply_reduce_fusion.4
  169.0 2.1 fusion.16
  172.2 0.8 fusion.24
  173.0 210.5 %reduce-scatter.3.cloned.1.call-done = f32[8,256]{1,0:T(8,128)} async-done(((f32[256,256]{1,0:T(8,128)}), f32[8,256]{1,0:T(8,128)}) %reduce-scatter.3.cloned.1.call-update) | async-done | bytes 8208 | tf_op jit(solution)/shard_map/reduce_scatter | solution.py:93
  383.5 1.0 fusion.60
  384.6 83.0 %all-reduce.6 = bf16[512,256]{1,0:T(8,128)(2,1)S(1)} all-reduce(f32[512,256]{1,0:T(8,128)S(1)} %fusion.60), channel_id=1, replica_groups=mesh['rows'=8,'pts'=32] {'rows','pts'}, use_global_device_ids=true, to_apply=%region_7.8 | all-reduce | flops 131072 | bytes 786432 | tf_op jit(solution)/shard_map/psum | solution.py:96
  467.6 2.1 fusion.28
  469.8 1.2 gather_fusion.7
  471.1 98.4 %all-gather.3.cloned.1.call-done = bf16[2048,256]{1,0:T(8,128)(2,1)} async-done(((bf16[8,256]{1,0:T(8,128)(2,1)}), bf16[2048,256]{1,0:T(8,128)(2,1)}) %all-gather.3.cloned.1.call-update) | async-done | bytes 1048592 | tf_op jit(solution)/shard_map/all_gather | solution.py:98
  569.5 12.7 %scatter_custom_fusion.1 = f32[1024,256]{1,0:T(8,128)S(1)} fusion(f32[1024,256]{1,0:T(8,128)S(1)} %get-tuple-element.9, s32[2048]{0:T(1024)S(1)} %bitcast.54, bf16[2048,256]{1,0:T(8,128)(2,1)} %all-gather.3.cloned.1.call-done, f32[]{:T(128)} %constant.14.clone.1), kind=kCustom, calls=%fused_computation.19 | custom fusion | flops 1572864 | bytes 2097156 | tf_op jit(solution)/shard_map/scatter-add | solution.py:100
  582.2 13.8 %scatter_custom_fusion = f32[1024,256]{1,0:T(8,128)} fusion(f32[1024,256]{1,0:T(8,128)} %get-tuple-element.8, s32[2048]{0:T(1024)S(1)} %bitcast.55, bf16[2048,256]{1,0:T(8,128)(2,1)S(1)} %copy-done.3, f32[]{:T(128)} %constant.13.clone.1), kind=kCustom, calls=%fused_computation.18 | custom fusion | flops 1572864 | bytes 2097664 | tf_op jit(solution)/shard_map/scatter-add | solution.py:104
  596.0 2.5 multiply_add_fusion
  598.4 1.0 gather_fusion.6
  599.4 1.3 fusion.17
  601.2 206.7 %reduce-scatter.5.cloned.1.call-done = f32[8,256]{1,0:T(8,128)} async-done(((f32[256,256]{1,0:T(8,128)}), f32[8,256]{1,0:T(8,128)}) %reduce-scatter.5.cloned.1.call-update) | async-done | bytes 8208 | tf_op jit(solution)/shard_map/reduce_scatter | solution.py:93
  807.9 1.0 fusion.58
  808.9 82.9 %all-reduce.7 = bf16[512,256]{1,0:T(8,128)(2,1)S(1)} all-reduce(f32[512,256]{1,0:T(8,128)S(1)} %fusion.58), channel_id=1, replica_groups=mesh['rows'=8,'pts'=32] {'rows','pts'}, use_global_device_ids=true, to_apply=%region_16.17 | all-reduce | flops 131072 | bytes 786432 | tf_op jit(solution)/shard_map/psum | solution.py:96
  891.9 2.1 fusion.29
  894.0 99.8 %all-gather.5.cloned.1.call-done = bf16[2048,256]{1,0:T(8,128)(2,1)} async-done(((bf16[8,256]{1,0:T(8,128)(2,1)}), bf16[2048,256]{1,0:T(8,128)(2,1)}) %all-gather.5.cloned.1.call-update) | async-done | bytes 1048592 | tf_op jit(solution)/shard_map/all_gather | solution.py:98
  993.8 12.5 %scatter_custom_fusion.2 = f32[1024,256]{1,0:T(8,128)S(1)} fusion(f32[1024,256]{1,0:T(8,128)S(1)} %get-tuple-element.7, s32[2048]{0:T(1024)S(1)} %bitcast.52, bf16[2048,256]{1,0:T(8,128)(2,1)} %all-gather.5.cloned.1.call-done, f32[]{:T(128)} %constant.14.clone.1), kind=kCustom, calls=%fused_computation.20 | custom fusion | flops 1572864 | bytes 2097156 | tf_op jit(solution)/shard_map/scatter-add | solution.py:100
  1006.3 14.1 %scatter_custom_fusion.3 = f32[1024,256]{1,0:T(8,128)} fusion(f32[1024,256]{1,0:T(8,128)} %get-tuple-element.6, s32[2048]{0:T(1024)S(1)} %bitcast.53, bf16[2048,256]{1,0:T(8,128)(2,1)S(1)} %copy-done.4, f32[]{:T(128)} %constant.13.clone.1), kind=kCustom, calls=%fused_computation.21 | custom fusion | flops 1572864 | bytes 2097664 | tf_op jit(solution)/shard_map/scatter-add | solution.py:104
  (59 shorter events, 6.0 us)
Async XLA Ops:
  7.2 19.2 %copy-start = (bf16[1024,256]{1,0:T(8,128)(2,1)S(1)}, bf16[1024,256]{1,0:T(8,128)(2,1)}, u32[]{:S(2)}) copy-start(bf16[1024,256]{1,0:T(8,128)(2,1)} %param.8) | copy-start | bytes 1572868
  7.2 160.9 %all-reduce.5.cloned.1.call-start = ((), (), s32[]{:S(2)}) async-start(), calls=%async_computation.6 | async-start | bytes 786432 | tf_op jit(solution)/shard_map/psum | solution.py:78
  12.1 3.2 copy-start.1
  18.4 4.5 copy-start.5
  22.8 360.7 %reduce-scatter.3.cloned.1.call-start = ((), (), s32[]{:S(2)}) async-start(), calls=%async_computation.2 | async-start | bytes 270336 | tf_op jit(solution)/shard_map/reduce_scatter | solution.py:93
  169.0 3.0 copy-start.7
  171.2 398.3 %all-gather.3.cloned.1.call-start = ((), (), s32[]{:S(2)}) async-start(), calls=%async_computation.3 | async-start | bytes 1052672 | tf_op jit(solution)/shard_map/all_gather | solution.py:98
  383.5 84.0 %copy-start.10 = (f32[8,256]{1,0:T(8,128)S(1)}, f32[8,256]{1,0:T(8,128)}, u32[]{:S(2)}) copy-start(f32[8,256]{1,0:T(8,128)} %reduce-scatter.3.cloned.1.call-done) | copy-start | bytes 24580
  467.5 3.4 copy-start.9
  467.5 3.4 copy-start.8
  469.7 338.1 %reduce-scatter.5.cloned.1.call-start = ((), (), s32[]{:S(2)}) async-start(), calls=%async_computation.4 | async-start | bytes 270336 | tf_op jit(solution)/shard_map/reduce_scatter | solution.py:93
  569.5 12.7 %copy-start.3 = (bf16[2048,256]{1,0:T(8,128)(2,1)S(1)}, bf16[2048,256]{1,0:T(8,128)(2,1)}, u32[]{:S(2)}) copy-start(bf16[2048,256]{1,0:T(8,128)(2,1)} %all-gather.3.cloned.1.call-done) | copy-start | bytes 3145732
  599.4 1.5 copy-start.6
  600.7 393.1 %all-gather.5.cloned.1.call-start = ((), (), s32[]{:S(2)}) async-start(), calls=%async_computation.5 | async-start | bytes 1052672 | tf_op jit(solution)/shard_map/all_gather | solution.py:98
  807.9 84.0 %copy-start.11 = (f32[8,256]{1,0:T(8,128)S(1)}, f32[8,256]{1,0:T(8,128)}, u32[]{:S(2)}) copy-start(f32[8,256]{1,0:T(8,128)} %reduce-scatter.5.cloned.1.call-done) | copy-start | bytes 24580
  993.8 12.5 %copy-start.4 = (bf16[2048,256]{1,0:T(8,128)(2,1)S(1)}, bf16[2048,256]{1,0:T(8,128)(2,1)}, u32[]{:S(2)}) copy-start(bf16[2048,256]{1,0:T(8,128)(2,1)} %all-gather.5.cloned.1.call-done) | copy-start | bytes 3145732
  1006.3 14.2 %copy-start.2 = (f32[1024,256]{1,0:T(8,128)}, f32[1024,256]{1,0:T(8,128)S(1)}, u32[]{:S(2)}) copy-start(f32[1024,256]{1,0:T(8,128)S(1)} %scatter_custom_fusion.2) | copy-start | bytes 3145732
Sparse Core Ops, SparseCore 0:
  22.9 145.1 all-reduce.4
  172.9 210.5 reduce-scatter.2
  469.8 99.5 all-gather.2
  600.8 206.9 reduce-scatter.4
  894.1 99.5 all-gather.4
where the time goes:
time: 1030 us
  waiting for transfers between devices  756 us (73%)
  blocking collectives  166 us (16%)
  other arithmetic  64.6 us (6%)
  local copies, waits for them, and re-layouts  15.8 us (2%)
  between operations  14.1 us (1%)
  matrix products  10.7 us (1%)
    reduce_scatter x2, waiting for transfers between devices, shards(): lax.psum_scatter(partial_value, 'pts', scatter_dimension=0, tiled=True)  417 us
    all_gather x2, waiting for transfers between devices, shards(): steps = lax.all_gather(step_bf, ('rows', 'pts'), axis=0, tiled=True)  198 us
    psum x2, blocking collectives, shards(): proj = lax.psum(project_rows(factor, resid), ('rows', 'pts'))  166 us
    psum x1, waiting for transfers between devices, shards(): lax.psum(row_terms, 'pts').astype(jnp.float32)  140 us
    scatter-add x2, other arithmetic, shards(): momentum_now = (beta_keep * momentum_now + (1.0 - beta_keep) * mixed).at[...  27.9 us
    scatter-add x2, other arithmetic, shards(): current = mixed.at[whole_slots].add(-step_size * change, mode='drop')  25.2 us
  transfers between devices with their start and end apart: 5, of which 5 were waited for; matrix products, arithmetic and copies ran while one was open for 1% of the time, Pallas kernels for 0%

commit v1 on v0

--- a/solution.py
+++ b/solution.py
@@ -1,3 +1,4 @@
+import functools
 import jax
 import jax.numpy as jnp
 from jax import lax
@@ -9,6 +10,14 @@
 step_size = 0.2
 momentum_gain = 1.5
 ridge_term = 1.0
+
+
+def open_threads_on(vector, mesh_dim):
+    carry_in = jnp.sum(lax.all_gather(vector, mesh_dim), axis=0)
+    return carry_in
+
+
+pack_points_on = functools.partial(open_threads_on, mesh_dim="pts")
 
 
 def kernel_tile(left_rows, right_rows):
@@ -75,7 +84,7 @@
             pivot_holder[:, None], features[pivot_pos], jnp.zeros((), jnp.bfloat16)
         )
         got_rows, got_pivots = (
-            lax.psum(row_terms, "pts").astype(jnp.float32),
+            pack_points_on(row_terms).astype(jnp.float32),
             lax.psum(pivot_terms, "pts").astype(jnp.float32),
         )
         block_feats = got_rows.astype(jnp.bfloat16)

time: 1030 us -> 1100 us (1.068)
  waiting for transfers between devices: 756 us -> 819 us
    all_gather x0 -> x2, waiting for transfers between devices: none -> 62 us  [open_threads_on(): carry_in = jnp.sum(lax.all_gather(vector, mesh_dim), axis=0)]
  transfers between devices with their start and end apart: 5 -> 7, of which waited for: 5 -> 6; matrix products, arithmetic and copies ran while one was open for 1% -> 3% of each run, Pallas kernels for 0% -> 0%
where the time goes in v1:
time: 1100 us; the launch traced here: 1090 us
  waiting for transfers between devices  819 us (74%)
  blocking collectives  166 us (15%)
  other arithmetic  67.9 us (6%)
  local copies, waits for them, and re-layouts  16.6 us (2%)
  between operations  14.4 us (1%)
    reduce_scatter x2, waiting for transfers between devices, shards(): lax.psum_scatter(partial_value, 'pts', scatter_dimension=0, tiled=True)  419 us
    all_gather x2, waiting for transfers between devices, shards(): steps = lax.all_gather(step_bf, ('rows', 'pts'), axis=0, tiled=True)  199 us
    psum x2, blocking collectives, shards(): proj = lax.psum(project_rows(factor, resid), ('rows', 'pts'))  166 us
    psum x1, waiting for transfers between devices, shards(): lax.psum(pivot_terms, 'pts').astype(jnp.float32)  139 us
    all_gather x2, waiting for transfers between devices, open_threads_on(): carry_in = jnp.sum(lax.all_gather(vector, mesh_dim), axis=0)  62 us
    scatter-add x2, other arithmetic, shards(): momentum_now = (beta_keep * momentum_now + (1.0 - beta_keep) * mixed).at[...  27.9 us
    scatter-add x2, other arithmetic, shards(): current = mixed.at[whole_slots].add(-step_size * change, mode='drop')  25.2 us
  transfers between devices with their start and end apart: 7, of which 6 were waited for; matrix products, arithmetic and copies ran while one was open for 3% of the time, Pallas kernels for 0%

profile of v1, /device:TPU:1, one launch (start us, length us, event | category | flops | bytes accessed | tf_op | source)
XLA Modules:
  0.0 1094.7 jit_solution(5457746668767336909)
XLA Ops:
  8.1 1.7 gather_fusion
  11.4 3.1 gather_fusion.8
  14.6 3.1 gather_fusion.3
  17.8 1.3 gather_fusion.4
  19.2 1.3 gather_fusion.9
  22.4 2.6 multiply_add_fusion.2
  25.0 1.0 gather_fusion.1
  25.9 1.2 gather_fusion.2
  27.1 62.0 %all-gather.5.cloned.1.call-done = bf16[32,256,128]{2,1,0:T(8,128)(2,1)} async-done(((bf16[1,256,128]{2,1,0:T(8,128)(2,1)}), bf16[32,256,128]{2,1,0:T(8,128)(2,1)}) %all-gather.5.cloned.1.call-update) | async-done | bytes 2097168 | tf_op jit(solution)/shard_map/all_gather | solution.py:16
  89.1 1.9 reduce_sum.91
  91.1 1.3 fusion.16
  94.1 139.4 %all-reduce.5.cloned.1.call-done = (bf16[512,128]{1,0:T(8,128)(2,1)}, bf16[512,128]{1,0:T(8,128)(2,1)}) async-done(((bf16[512,128]{1,0:T(8,128)(2,1)}, bf16[512,128]{1,0:T(8,128)(2,1)}), (bf16[512,128]{1,0:T(8,128)(2,1)}, bf16[512,128]{1,0:T(8,128)(2,1)})) %all-reduce.5.cloned.1.call-update) | async-done | bytes 262160 | tf_op jit(solution)/shard_map/psum | solution.py:88
  233.5 1.0 multiply_reduce_fusion.2
  234.7 1.1 fusion.24
  235.8 212.3 %reduce-scatter.3.cloned.1.call-done = f32[8,256]{1,0:T(8,128)} async-done(((f32[256,256]{1,0:T(8,128)}), f32[8,256]{1,0:T(8,128)}) %reduce-scatter.3.cloned.1.call-update) | async-done | bytes 8208 | tf_op jit(solution)/shard_map/reduce_scatter | solution.py:102
  448.1 1.0 fusion.60
  449.0 83.4 %all-reduce.6 = bf16[512,256]{1,0:T(8,128)(2,1)S(1)} all-reduce(f32[512,256]{1,0:T(8,128)S(1)} %fusion.60), channel_id=1, replica_groups=mesh['rows'=8,'pts'=32] {'rows','pts'}, use_global_device_ids=true, to_apply=%region_7.8 | all-reduce | flops 131072 | bytes 786432 | tf_op jit(solution)/shard_map/psum | solution.py:105
  532.5 2.1 fusion.28
  534.6 1.2 gather_fusion.7
  535.9 1.9 reduce_sum.96
  537.9 98.9 %all-gather.7.cloned.1.call-done = bf16[2048,256]{1,0:T(8,128)(2,1)} async-done(((bf16[8,256]{1,0:T(8,128)(2,1)}), bf16[2048,256]{1,0:T(8,128)(2,1)}) %all-gather.7.cloned.1.call-update) | async-done | bytes 1048592 | tf_op jit(solution)/shard_map/all_gather | solution.py:107
  636.8 12.7 %scatter_custom_fusion.1 = f32[1024,256]{1,0:T(8,128)S(1)} fusion(f32[1024,256]{1,0:T(8,128)S(1)} %get-tuple-element.7, s32[2048]{0:T(1024)S(1)} %bitcast.58, bf16[2048,256]{1,0:T(8,128)(2,1)} %all-gather.7.cloned.1.call-done, f32[]{:T(128)} %constant.16.clone.1), kind=kCustom, calls=%fused_computation.19 | custom fusion | flops 1572864 | bytes 2097156 | tf_op jit(solution)/shard_map/scatter-add | solution.py:109
  649.6 13.8 %scatter_custom_fusion = f32[1024,256]{1,0:T(8,128)} fusion(f32[1024,256]{1,0:T(8,128)} %get-tuple-element.6, s32[2048]{0:T(1024)S(1)} %bitcast.59, bf16[2048,256]{1,0:T(8,128)(2,1)S(1)} %copy-done.3, f32[]{:T(128)} %constant.15.clone.1), kind=kCustom, calls=%fused_computation.18 | custom fusion | flops 1572864 | bytes 2097664 | tf_op jit(solution)/shard_map/scatter-add | solution.py:113
  663.3 2.6 multiply_add_fusion
  665.9 1.0 gather_fusion.6
  666.9 1.3 fusion.17
  668.6 206.6 %reduce-scatter.5.cloned.1.call-done = f32[8,256]{1,0:T(8,128)} async-done(((f32[256,256]{1,0:T(8,128)}), f32[8,256]{1,0:T(8,128)}) %reduce-scatter.5.cloned.1.call-update) | async-done | bytes 8208 | tf_op jit(solution)/shard_map/reduce_scatter | solution.py:102
  876.2 83.0 %all-reduce.7 = bf16[512,256]{1,0:T(8,128)(2,1)S(1)} all-reduce(f32[512,256]{1,0:T(8,128)S(1)} %fusion.58), channel_id=1, replica_groups=mesh['rows'=8,'pts'=32] {'rows','pts'}, use_global_device_ids=true, to_apply=%region_16.17 | all-reduce | flops 131072 | bytes 786432 | tf_op jit(solution)/shard_map/psum | solution.py:105
  959.2 2.1 fusion.29
  961.3 99.8 %all-gather.11.cloned.1.call-done = bf16[2048,256]{1,0:T(8,128)(2,1)} async-done(((bf16[8,256]{1,0:T(8,128)(2,1)}), bf16[2048,256]{1,0:T(8,128)(2,1)}) %all-gather.11.cloned.1.call-update) | async-done | bytes 1048592 | tf_op jit(solution)/shard_map/all_gather | solution.py:107
  1061.2 12.5 %scatter_custom_fusion.2 = f32[1024,256]{1,0:T(8,128)S(1)} fusion(f32[1024,256]{1,0:T(8,128)S(1)} %get-tuple-element.5, s32[2048]{0:T(1024)S(1)} %bitcast.56, bf16[2048,256]{1,0:T(8,128)(2,1)} %all-gather.11.cloned.1.call-done, f32[]{:T(128)} %constant.16.clone.1), kind=kCustom, calls=%fused_computation.20 | custom fusion | flops 1572864 | bytes 2097156 | tf_op jit(solution)/shard_map/scatter-add | solution.py:109
  1073.7 14.1 %scatter_custom_fusion.3 = f32[1024,256]{1,0:T(8,128)} fusion(f32[1024,256]{1,0:T(8,128)} %get-tuple-element.4, s32[2048]{0:T(1024)S(1)} %bitcast.57, bf16[2048,256]{1,0:T(8,128)(2,1)S(1)} %copy-done.4, f32[]{:T(128)} %constant.15.clone.1), kind=kCustom, calls=%fused_computation.21 | custom fusion | flops 1572864 | bytes 2097664 | tf_op jit(solution)/shard_map/scatter-add | solution.py:113
  (61 shorter events, 8.1 us)
Async XLA Ops:
  7.2 18.8 %copy-start = (bf16[1024,256]{1,0:T(8,128)(2,1)S(1)}, bf16[1024,256]{1,0:T(8,128)(2,1)}, u32[]{:S(2)}) copy-start(bf16[1024,256]{1,0:T(8,128)(2,1)} %param.8) | copy-start | bytes 1572868
  7.2 81.9 %all-gather.5.cloned.1.call-start = ((), (), s32[]{:S(2)}) async-start(), calls=%async_computation.2 | async-start | bytes 2162688 | tf_op jit(solution)/shard_map/all_gather | solution.py:16
  10.6 222.9 %all-reduce.5.cloned.1.call-start = ((), (), s32[]{:S(2)}) async-start(), calls=%async_computation.8 | async-start | bytes 524288 | tf_op jit(solution)/shard_map/psum | solution.py:88
  11.4 6.4 copy-start.1
  17.7 4.7 copy-start.5
  22.1 425.9 %reduce-scatter.3.cloned.1.call-start = ((), (), s32[]{:S(2)}) async-start(), calls=%async_computation.3 | async-start | bytes 270336 | tf_op jit(solution)/shard_map/reduce_scatter | solution.py:102
  92.4 443.5 %all-gather.9.cloned.1.call-start = ((), (), s32[]{:S(2)}) async-start(), calls=%async_computation.5 | async-start | bytes 2162688 | tf_op jit(solution)/shard_map/all_gather | solution.py:16
  93.3 442.5 %copy-start.7 = (s32[2,2048]{1,0:T(2,128)S(1)}, s32[2,2048]{1,0:T(2,128)}, u32[]{:S(2)}) copy-start(s32[2,2048]{1,0:T(2,128)} %param.11) | copy-start | bytes 49156
  94.1 542.8 %all-gather.7.cloned.1.call-start = ((), (), s32[]{:S(2)}) async-start(), calls=%async_computation.4 | async-start | bytes 1052672 | tf_op jit(solution)/shard_map/all_gather | solution.py:107
  534.6 340.7 %reduce-scatter.5.cloned.1.call-start = ((), (), s32[]{:S(2)}) async-start(), calls=%async_computation.6 | async-start | bytes 270336 | tf_op jit(solution)/shard_map/reduce_scatter | solution.py:102
  636.8 12.7 %copy-start.3 = (bf16[2048,256]{1,0:T(8,128)(2,1)S(1)}, bf16[2048,256]{1,0:T(8,128)(2,1)}, u32[]{:S(2)}) copy-start(bf16[2048,256]{1,0:T(8,128)(2,1)} %all-gather.7.cloned.1.call-done) | copy-start | bytes 3145732
  665.9 2.3 copy-start.6
  668.1 393.0 %all-gather.11.cloned.1.call-start = ((), (), s32[]{:S(2)}) async-start(), calls=%async_computation.7 | async-start | bytes 1052672 | tf_op jit(solution)/shard_map/all_gather | solution.py:107
  1061.2 12.5 %copy-start.4 = (bf16[2048,256]{1,0:T(8,128)(2,1)S(1)}, bf16[2048,256]{1,0:T(8,128)(2,1)}, u32[]{:S(2)}) copy-start(bf16[2048,256]{1,0:T(8,128)(2,1)} %all-gather.11.cloned.1.call-done) | copy-start | bytes 3145732
  1073.7 14.2 %copy-start.2 = (f32[1024,256]{1,0:T(8,128)}, f32[1024,256]{1,0:T(8,128)S(1)}, u32[]{:S(2)}) copy-start(f32[1024,256]{1,0:T(8,128)S(1)} %scatter_custom_fusion.2) | copy-start | bytes 3145732
Sparse Core Ops, SparseCore 0:
  11.2 77.8 all-gather.4
  92.6 140.8 all-reduce.4
  237.9 210.1 reduce-scatter.2
  450.8 77.5 all-gather.8
  534.7 102.0 all-gather.6
  668.3 206.9 reduce-scatter.4
  961.5 99.6 all-gather.10
